TPU v7x, 128 devices: a whole 4x4x4 slice. The times are simulated.
128 devices in a mesh: fsdp: 64 (over z, x_hi, y, core), tensor: 2 (over x_lo).
Axes of the slice: x: 4 (x_hi: 2, x_lo: 2; x = x_hi * 2 + x_lo), y: 4, z: 4, core: 2. Of those that a mesh axis runs over, the one named last changes fastest.
Arguments:
- tokens: bfloat16 [8192, 1024], P('fsdp'), may hold values from -6 to 6
- segment: int32 [8192], P('fsdp'), may hold values from 0 to 8191, as said below
- w_query: bfloat16 [1024, 1024], P('fsdp', 'tensor'), may hold values from -0.1875 to 0.1875
- w_key: bfloat16 [1024, 512], P('fsdp', 'tensor'), may hold values from -0.1875 to 0.1875
- w_value: bfloat16 [1024, 512], P('fsdp', 'tensor'), may hold values from -0.1875 to 0.1875
- w_output: bfloat16 [1024, 1024], P('tensor', 'fsdp'), may hold values from -0.5 to 0.5
- w_gate: bfloat16 [1024, 4608], P('fsdp', 'tensor'), may hold values from -0.1875 to 0.1875
- w_up: bfloat16 [1024, 4608], P('fsdp', 'tensor'), may hold values from -0.1875 to 0.1875
- w_down: bfloat16 [4608, 1024], P('tensor', 'fsdp'), may hold values from -0.09375 to 0.09375
- norm_attn: bfloat16 [1024], P('fsdp'), may hold values from 0.25 to 1.75
- norm_ffn: bfloat16 [1024], P('fsdp'), may hold values from 0.25 to 1.75
- norm_query: bfloat16 [64], P('fsdp'), may hold values from 0.25 to 1.75
- norm_key: bfloat16 [64], P('fsdp'), may hold values from 0.25 to 1.75
- cotangent: bfloat16 [8192, 1024], P('fsdp'), may hold values from -16 to 16
Outputs:
- block_out: bfloat16 [8192, 1024], P('fsdp')
- grad_tokens: bfloat16 [8192, 1024], P('fsdp')
- grad_query: float32 [1024, 1024], P('fsdp', 'tensor')
- grad_key: float32 [1024, 512], P('fsdp', 'tensor')
- grad_value: float32 [1024, 512], P('fsdp', 'tensor')
- grad_output: float32 [1024, 1024], P('tensor', 'fsdp')
- grad_gate: float32 [1024, 4608], P('fsdp', 'tensor')
- grad_up: float32 [1024, 4608], P('fsdp', 'tensor')
- grad_down: float32 [4608, 1024], P('tensor', 'fsdp')
- grad_norm_attn: float32 [1024], P('fsdp')
- grad_norm_ffn: float32 [1024], P('fsdp')
- grad_norm_query: float32 [64], P('fsdp')
- grad_norm_key: float32 [64], P('fsdp')
Inputs may be any that keep to these rules, and one draw needn't show every extreme that they name: `segment`: ids never fall; all tokens of an id lie in one aligned block of 128 tokens; the first and the last token of every such block start a new id.
All inputs are finite; a program needn't handle non-finite values.
Results may differ from a plain program's by a relative error of at most 0.019.
Values may be sent and summed in bfloat16 or wider, within the bound.
No kernel may reach another device: no remote copies, remote signals or barrier semaphores. Data moves between devices by JAX's collectives and lax.ppermute only.
A program may use at most 128 MiB of HBM per device.

v0:
```python
import jax
import jax.numpy as jnp
from jax import lax
from jax.sharding import PartitionSpec as P

epsilon = 1e-05
rope_base = 1000000.0


def matmul(matrix, second):
    return jnp.dot(matrix, second, preferred_element_type=jnp.float32)


def matmul_tr(matrix, second):
    return lax.dot_general(
        matrix, second, (((1,), (1,)), ((), ())), preferred_element_type=jnp.float32
    )


def tr_matmul(matrix, second):
    return lax.dot_general(
        matrix, second, (((0,), (0,)), ((), ())), preferred_element_type=jnp.float32
    )


def contract(pattern, matrix, second):
    return jnp.einsum(pattern, matrix, second, preferred_element_type=jnp.float32)


def normalize(vector):
    inverse = lax.rsqrt(jnp.mean(vector * vector, axis=-1, keepdims=True) + epsilon)
    return (vector * inverse, inverse)


def norm_back(grad_in, normed, inverse):
    return inverse * (grad_in - normed * jnp.mean(grad_in * normed, axis=-1, keepdims=True))


def rotate(vector):
    half_size = vector.shape[-1] // 2
    return jnp.concatenate([-vector[..., half_size:], vector[..., :half_size]], axis=-1)


def rotate_back(vector):
    half_size = vector.shape[-1] // 2
    return jnp.concatenate([vector[..., half_size:], -vector[..., :half_size]], axis=-1)


def tables(segment, head_size):
    row_count = segment.shape[0]
    row_index = jnp.arange(row_count, dtype=jnp.int32)
    same_segment = segment[:, None] == segment[None, :]
    first_row = jnp.min(jnp.where(same_segment, row_index[None, :], row_count), axis=1)
    position = (row_index - first_row).astype(jnp.float32)
    allowed = same_segment & (row_index[None, :] <= row_index[:, None])
    half_size = head_size // 2
    frequency = jnp.power(rope_base, -2.0 * jnp.arange(half_size, dtype=jnp.float32) / head_size)
    phase_angle = position[:, None] * frequency[None, :]
    phase_angle = jnp.concatenate([phase_angle, phase_angle], axis=1)
    return (allowed, jnp.cos(phase_angle)[:, None, :], jnp.sin(phase_angle)[:, None, :])


def head_prep(raw_heads, head_gain, cos_table, sin_table):
    unit_heads, inverse = normalize(raw_heads)
    scaled = unit_heads * head_gain
    return (scaled * cos_table + rotate(scaled) * sin_table, unit_heads, inverse)


def head_back(grad_in, unit_heads, inverse, head_gain, cos_table, sin_table):
    grad_scaled = grad_in * cos_table + rotate_back(grad_in * sin_table)
    gain_grad = jnp.sum(grad_scaled * unit_heads, axis=(0, 1))
    return (norm_back(grad_scaled * head_gain, unit_heads, inverse), gain_grad)


def score_block(query_heads, key_heads, allowed):
    row_count, head_count, head_size = query_heads.shape
    kv_count = key_heads.shape[1]
    query_groups = query_heads.reshape(row_count, kv_count, head_count // kv_count, head_size)
    scores = contract("ikgd,jkd->kgij", query_groups, key_heads) * head_size ** (-0.5)
    return (query_groups, jnp.where(allowed, scores, -1e30))


def attend(query_heads, key_heads, value_heads, allowed):
    row_count, head_count, head_size = query_heads.shape
    query_groups, masked = score_block(query_heads, key_heads, allowed)
    row_max = jnp.max(masked, axis=-1, keepdims=True)
    exp_scores = jnp.exp(masked - row_max)
    denominator = jnp.sum(exp_scores, axis=-1, keepdims=True)
    log_total = row_max + jnp.log(denominator)
    attn_weights = (exp_scores / denominator).astype(jnp.bfloat16)
    mixed = contract("kgij,jkd->ikgd", attn_weights, value_heads).astype(jnp.bfloat16)
    return (mixed.reshape(row_count, head_count * head_size), log_total)


def attend_back(query_heads, key_heads, value_heads, attended, grad_attended, log_total, allowed):
    row_count, head_count, head_size = query_heads.shape
    kv_count = key_heads.shape[1]
    group_size = head_count // kv_count
    query_groups, masked = score_block(query_heads, key_heads, allowed)
    prob = jnp.exp(masked - log_total)
    prob_low = prob.astype(jnp.bfloat16)
    grad_groups = grad_attended.reshape(row_count, kv_count, group_size, head_size)
    out_groups = attended.reshape(row_count, kv_count, group_size, head_size)
    row_delta = jnp.sum(grad_groups.astype(jnp.float32) * out_groups.astype(jnp.float32), axis=-1)
    row_delta = jnp.transpose(row_delta, (1, 2, 0))[..., None]
    grad_kv_value = contract("kgij,ikgd->jkd", prob_low, grad_groups)
    grad_prob = contract("ikgd,jkd->kgij", grad_groups, value_heads)
    grad_scores = (prob * (grad_prob - row_delta) * head_size ** (-0.5)).astype(jnp.bfloat16)
    grad_query = contract("kgij,jkd->ikgd", grad_scores, key_heads).reshape(
        row_count, head_count, head_size
    )
    grad_key = contract("kgij,ikgd->jkd", grad_scores, query_groups)
    return (grad_query, grad_key, grad_kv_value)


def on_device(
    tokens,
    segment,
    w_query,
    w_key,
    w_value,
    w_output,
    w_gate,
    w_up,
    w_down,
    norm_attn,
    norm_ffn,
    norm_query,
    norm_key,
    cotangent,
):
    shards = (
        w_query,
        w_key,
        w_value,
        w_gate,
        w_up,
        w_output,
        w_down,
        norm_attn,
        norm_ffn,
        norm_query,
        norm_key,
    )
    gathered = (
        lax.all_gather(shards[0], "fsdp", axis=0, tiled=True),
        lax.all_gather(shards[1], "fsdp", axis=0, tiled=True),
        lax.all_gather(shards[2], "fsdp", axis=0, tiled=True),
        lax.all_gather(shards[3], "fsdp", axis=0, tiled=True),
        lax.all_gather(shards[4], "fsdp", axis=0, tiled=True),
        lax.all_gather(shards[5], "fsdp", axis=1, tiled=True),
        lax.all_gather(shards[6], "fsdp", axis=1, tiled=True),
        lax.all_gather(shards[7], "fsdp", axis=0, tiled=True),
        lax.all_gather(shards[8], "fsdp", axis=0, tiled=True),
        lax.all_gather(shards[9], "fsdp", axis=0, tiled=True),
        lax.all_gather(shards[10], "fsdp", axis=0, tiled=True),
    )
    (
        full_query,
        full_key,
        full_value,
        full_gate,
        full_up,
        full_output,
        full_down,
        gain_attn,
        gain_ffn,
        gain_query,
        gain_key,
    ) = gathered
    row_count = tokens.shape[0]
    head_size = gain_query.shape[0]
    head_count = full_query.shape[1] // head_size
    kv_count = full_key.shape[1] // head_size
    allowed, cos_table, sin_table = tables(segment, head_size)
    inputs = tokens.astype(jnp.float32)
    normed_one, inv_one = normalize(inputs)
    hidden_one = (normed_one * gain_attn).astype(jnp.bfloat16)
    query_raw = matmul(hidden_one, full_query).reshape(row_count, head_count, head_size)
    key_raw = matmul(hidden_one, full_key).reshape(row_count, kv_count, head_size)
    value_heads = (
        matmul(hidden_one, full_value).astype(jnp.bfloat16).reshape(row_count, kv_count, head_size)
    )
    query_rot, query_unit, query_inv = head_prep(query_raw, gain_query, cos_table, sin_table)
    key_rot, key_unit, key_inv = head_prep(key_raw, gain_key, cos_table, sin_table)
    query_heads = query_rot.astype(jnp.bfloat16)
    key_heads = key_rot.astype(jnp.bfloat16)
    attended, log_total = attend(query_heads, key_heads, value_heads, allowed)
    residual = inputs + lax.psum(matmul(attended, full_output), "tensor")
    normed_two, inv_two = normalize(residual)
    hidden_two = (normed_two * gain_ffn).astype(jnp.bfloat16)
    gate_pre = matmul(hidden_two, full_gate)
    up_pre = matmul(hidden_two, full_up)
    sigmoid_gate = jax.nn.sigmoid(gate_pre)
    activation = (gate_pre * sigmoid_gate * up_pre).astype(jnp.bfloat16)
    ffn_result = lax.psum(matmul(activation, full_down).astype(jnp.bfloat16), "tensor").astype(
        jnp.float32
    )
    block_out = (residual + ffn_result).astype(jnp.bfloat16)
    (
        back_query,
        back_key,
        back_value,
        back_gate,
        back_up,
        back_output,
        back_down,
        back_attn,
        back_ffn,
        back_qgain,
        back_kgain,
    ) = gathered
    grad_act = matmul_tr(cotangent, back_down)
    grad_gate_pre = (
        grad_act * up_pre * sigmoid_gate * (1.0 + gate_pre * (1.0 - sigmoid_gate))
    ).astype(jnp.bfloat16)
    grad_up_pre = (grad_act * gate_pre * sigmoid_gate).astype(jnp.bfloat16)
    partial_two = matmul_tr(grad_gate_pre, back_gate) + matmul_tr(grad_up_pre, back_up)
    grad_hidden_two = lax.psum(partial_two, "tensor")
    grad_norm_ffn = jnp.sum(grad_hidden_two * normed_two, axis=0)
    ffn_width = grad_gate_pre.shape[1]
    grad_residual = cotangent.astype(jnp.float32) + norm_back(
        grad_hidden_two * back_ffn, normed_two, inv_two
    )
    grad_res_low = grad_residual.astype(jnp.bfloat16)
    grad_attended = matmul_tr(grad_res_low, back_output).astype(jnp.bfloat16)
    grad_q_rot, grad_k_rot, grad_kv_value = attend_back(
        query_heads, key_heads, value_heads, attended, grad_attended, log_total, allowed
    )
    grad_q_raw, part_norm_query = head_back(
        grad_q_rot, query_unit, query_inv, back_qgain, cos_table, sin_table
    )
    grad_k_raw, part_norm_key = head_back(
        grad_k_rot, key_unit, key_inv, back_kgain, cos_table, sin_table
    )
    query_low = grad_q_raw.reshape(row_count, head_count * head_size).astype(jnp.bfloat16)
    key_low = grad_k_raw.reshape(row_count, kv_count * head_size).astype(jnp.bfloat16)
    value_low = grad_kv_value.reshape(row_count, kv_count * head_size).astype(jnp.bfloat16)
    partial_one = (
        matmul_tr(query_low, back_query)
        + matmul_tr(key_low, back_key)
        + matmul_tr(value_low, back_value)
    )
    grad_hidden_one, grad_norm_query, grad_norm_key = lax.psum(
        (partial_one, part_norm_query, part_norm_key), "tensor"
    )
    grad_norm_attn = jnp.sum(grad_hidden_one * normed_one, axis=0)
    grad_tokens = (
        grad_residual + norm_back(grad_hidden_one * back_attn, normed_one, inv_one)
    ).astype(jnp.bfloat16)
    query_width = query_low.shape[1]
    key_width = key_low.shape[1]
    whole_owned = lax.psum_scatter(
        jnp.concatenate(
            [
                jnp.concatenate(
                    [
                        tr_matmul(hidden_one, query_low),
                        tr_matmul(hidden_one, key_low),
                        tr_matmul(hidden_one, value_low),
                        tr_matmul(grad_res_low, attended),
                    ],
                    axis=1,
                ),
                jnp.concatenate(
                    [
                        tr_matmul(hidden_two, grad_gate_pre),
                        tr_matmul(hidden_two, grad_up_pre),
                        tr_matmul(cotangent, activation),
                    ],
                    axis=1,
                ),
            ],
            axis=1,
        ),
        "fsdp",
        scatter_dimension=0,
        tiled=True,
    )
    attn_width = 2 * query_width + 2 * key_width
    attn_owned = whole_owned[:, :attn_width]
    ffn_owned = whole_owned[:, attn_width:]
    gain_owned = (
        lax.psum_scatter(grad_norm_attn, "fsdp", scatter_dimension=0, tiled=True),
        lax.psum_scatter(grad_norm_ffn, "fsdp", scatter_dimension=0, tiled=True),
        lax.psum_scatter(grad_norm_query, "fsdp", scatter_dimension=0, tiled=True),
        lax.psum_scatter(grad_norm_key, "fsdp", scatter_dimension=0, tiled=True),
    )
    grad_query = attn_owned[:, :query_width]
    grad_key = attn_owned[:, query_width : query_width + key_width]
    grad_value = attn_owned[:, query_width + key_width : query_width + 2 * key_width]
    grad_output = attn_owned[:, query_width + 2 * key_width :].T
    grad_gate = ffn_owned[:, :ffn_width]
    grad_up = ffn_owned[:, ffn_width : 2 * ffn_width]
    grad_down = ffn_owned[:, 2 * ffn_width :].T
    return (
        block_out,
        grad_tokens,
        grad_query,
        grad_key,
        grad_value,
        grad_output,
        grad_gate,
        grad_up,
        grad_down,
        gain_owned[0],
        gain_owned[1],
        gain_owned[2],
        gain_owned[3],
    )


def solution(mesh):
    return jax.shard_map(
        on_device,
        mesh=mesh,
        in_specs=(
            P("fsdp", None),
            P("fsdp"),
            P("fsdp", "tensor"),
            P("fsdp", "tensor"),
            P("fsdp", "tensor"),
            P("tensor", "fsdp"),
            P("fsdp", "tensor"),
            P("fsdp", "tensor"),
            P("tensor", "fsdp"),
            P("fsdp"),
            P("fsdp"),
            P("fsdp"),
            P("fsdp"),
            P("fsdp", None),
        ),
        out_specs=(
            P("fsdp", None),
            P("fsdp", None),
            P("fsdp", "tensor"),
            P("fsdp", "tensor"),
            P("fsdp", "tensor"),
            P("tensor", "fsdp"),
            P("fsdp", "tensor"),
            P("fsdp", "tensor"),
            P("tensor", "fsdp"),
            P("fsdp"),
            P("fsdp"),
            P("fsdp"),
            P("fsdp"),
        ),
        check_vma=False,
    )
```

profile of v0, /device:TPU:0, one launch (start us, length us, event | category | flops | bytes accessed | tf_op | source)
XLA Modules:
  0.0 1088.6 jit_solution(5932731994119234216)
XLA Ops:
  12.0 1.3 fusion.45
  17.2 173.2 %all-reduce.10 = (bf16[1024]{0:T(1024)(128)(2,1)S(1)}, bf16[64]{0:T(256)(128)(2,1)S(1)}, bf16[64]{0:T(256)(128)(2,1)S(1)}, bf16[1024]{0:T(1024)(128)(2,1)S(1)}) all-reduce(bf16[1024]{0:T(1024)(128)(2,1)S(1)} %dynamic-update-slice, bf16[64]{0:T(256)(128)(2,1)S(1)} %dynamic-update-slice.1, ...), channel_id=1, replica_groups=mesh['fsdp'=64,'tensor'=2] {'fsdp'}, use_global_device_ids=true, to_apply=%add | all-reduce | flops 2176 | bytes 8704
  190.6 89.9 %all_gather.35 = bf16[1024,256]{1,0:T(8,128)(2,1)S(1)} all-gather(bf16[16,256]{1,0:T(8,128)(2,1)} %param.17), channel_id=1, replica_groups=mesh['fsdp'=64,'tensor'=2] {'fsdp'}, dimensions={0}, use_global_device_ids=true | all-gather | bytes 532480 | tf_op jit(solution)/shard_map/all_gather | solution.py:147
  280.5 1.4 multiply_reduce_fusion.9
  282.0 91.7 %all_gather.34 = bf16[1024,256]{1,0:T(8,128)(2,1)S(1)} all-gather(bf16[16,256]{1,0:T(8,128)(2,1)} %param.18), channel_id=1, replica_groups=mesh['fsdp'=64,'tensor'=2] {'fsdp'}, dimensions={0}, use_global_device_ids=true | all-gather | bytes 532480 | tf_op jit(solution)/shard_map/all_gather | solution.py:148
  374.5 1.2 convolution_convert_fusion.3
  376.8 1.7 fusion.37
  379.6 2.5 fusion.47
  386.3 25.0 %all-reduce.16.cloned.1.call-done = f32[128,1024]{1,0:T(8,128)} async-done(((f32[128,1024]{1,0:T(8,128)}), f32[128,1024]{1,0:T(8,128)}) %all-reduce.16.cloned.1.call-update) | async-done | bytes 524304 | tf_op jit(solution)/shard_map/psum | solution.py:189
  411.3 1.2 multiply_reduce_fusion.2
  413.2 75.6 %all-gather.12.cloned.1.call-done = bf16[1024,2304]{1,0:T(8,128)(2,1)} async-done(((bf16[16,2304]{1,0:T(8,128)(2,1)}), bf16[1024,2304]{1,0:T(8,128)(2,1)}) %all-gather.12.cloned.1.call-update) | async-done | bytes 4718608 | tf_op jit(solution)/shard_map/all_gather | solution.py:150
  488.8 4.2 fusion.49
  492.9 70.8 %all-gather.10.cloned.1.call-done = bf16[1024,2304]{1,0:T(8,128)(2,1)} async-done(((bf16[16,2304]{1,0:T(8,128)(2,1)}), bf16[1024,2304]{1,0:T(8,128)(2,1)}) %all-gather.10.cloned.1.call-update) | async-done | bytes 4718608 | tf_op jit(solution)/shard_map/all_gather | solution.py:149
  563.7 4.1 fusion.48
  567.9 70.8 %all-gather.14.cloned.1.call-done = bf16[2304,1024]{0,1:T(8,128)(2,1)} async-done(((bf16[2304,16]{0,1:T(8,128)(2,1)}), bf16[2304,1024]{0,1:T(8,128)(2,1)}) %all-gather.14.cloned.1.call-update) | async-done | bytes 4718608 | tf_op jit(solution)/shard_map/all_gather | solution.py:152
  638.7 5.1 multiply_convert_fusion
  643.8 1.6 fusion.50
  645.5 4.8 convolution_add_fusion.1
  650.3 1.3 log_add_fusion
  651.6 4.9 convolution_convert_fusion
  656.8 27.3 %all-reduce.20.cloned.1.call-done = f32[128,1024]{1,0:T(8,128)} async-done(((f32[128,1024]{1,0:T(8,128)}), f32[128,1024]{1,0:T(8,128)}) %all-reduce.20.cloned.1.call-update) | async-done | bytes 524304 | tf_op jit(solution)/shard_map/psum | solution.py:219
  684.1 1.9 multiply_reduce_fusion
  686.5 31.4 %all-reduce.18.cloned.1.call-done = bf16[128,1024]{1,0:T(8,128)(2,1)} async-done(((bf16[128,1024]{1,0:T(8,128)(2,1)}), bf16[128,1024]{1,0:T(8,128)(2,1)}) %all-reduce.18.cloned.1.call-update) | async-done | bytes 262160 | tf_op jit(solution)/shard_map/psum | solution.py:196
  717.9 2.2 multiply_add_fusion
  720.0 1.5 convolution_convert_fusion.1
  723.6 1.1 fusion.6
  725.1 2.1 fusion.53
  727.3 1.4 multiply_reduce_fusion.7
  733.6 1.3 multiply_convert_fusion.4
  734.9 1.9 convolution_dynamic-update-slice_fusion.3
  736.8 2.5 fusion
  739.4 1.4 convolution_dynamic-update-slice_fusion.5
  740.8 2.3 convolution_dynamic-update-slice_fusion.4
  743.1 1.9 convolution_dynamic-update-slice_fusion.2
  745.0 5.1 convolution_dynamic-update-slice_fusion.1
  750.1 5.0 convolution_dynamic-update-slice_fusion
  755.2 5.1 bitcast_dynamic-update-slice_fusion
  760.3 15.3 %all-reduce.22.cloned.1.call-done = f32[128,1024]{1,0:T(8,128)} async-done(((f32[128,1024]{1,0:T(8,128)}), f32[128,1024]{1,0:T(8,128)}) %all-reduce.22.cloned.1.call-update) | async-done | bytes 524304 | tf_op jit(solution)/shard_map/psum | solution.py:244
  775.6 1.3 fusion.18
  777.0 174.7 %all-reduce.8 = (f32[1024]{0:T(1024)S(1)}, f32[1024]{0:T(1024)S(1)}, f32[64]{0:T(128)S(1)}, f32[64]{0:T(128)S(1)}) all-reduce(f32[1024]{0:T(1024)S(1)} %get-tuple-element.15, f32[1024]{0:T(1024)S(1)} %copy-done.19, f32[64]{0:T(128)S(1)} %get-tuple-element.17, f32[64]{0:T(128)S(1)} %copy-done.25), channel_id=3, replica_groups=mesh['fsdp'=64,'tensor'=2] {'fsdp'}, use_global_device_ids=true, to_apply=%region_18.19.clone | all-reduce | flops 2176 | bytes 17408
  951.7 1.2 dynamic-slice.11
  952.9 1.2 dynamic-slice.9
  954.8 5.6 all-reduce.9
  961.6 2.0 fusion.17
  963.6 113.6 %reduce-scatter.2.cloned.1.call-done = f32[16,8448]{1,0:T(8,128)} async-done(((f32[1024,8448]{1,0:T(8,128)}), f32[16,8448]{1,0:T(8,128)}) %reduce-scatter.2.cloned.1.call-update) | async-done | bytes 540688 | tf_op jit(solution)/shard_map/reduce_scatter | solution.py:253
  1077.2 1.3 fusion.42
  1078.5 1.4 slice_bitcast_fusion.1
  1079.9 1.8 slice_bitcast_fusion
  (138 shorter events, 23.9 us)
Async XLA Ops:
  7.2 369.6 %all-gather.6.cloned.1.call-start = ((), (), s32[]{:S(2)}) async-start(), calls=%async_computation.1 | async-start | bytes 1064960 | tf_op jit(solution)/shard_map/all_gather | solution.py:146
  7.9 371.7 %all-gather.8.cloned.1.call-start = ((), (), s32[]{:S(2)}) async-start(), calls=%async_computation.2 | async-start | bytes 1064960 | tf_op jit(solution)/shard_map/all_gather | solution.py:151
  8.7 402.7 %all-reduce.16.cloned.1.call-start = ((), (), s32[]{:S(2)}) async-start(), calls=%async_computation.3 | async-start | bytes 1048576 | tf_op jit(solution)/shard_map/psum | solution.py:189
  12.0 366.6 %copy-start.16 = (f32[128]{0:T(128)}, f32[128]{0:T(128)S(1)}, u32[]{:S(2)}) copy-start(f32[128]{0:T(128)S(1)} %add_rsqrt_fusion.3) | copy-start | bytes 1540
  190.4 188.4 %copy-start.20 = (f32[64]{0:T(128)}, f32[64]{0:T(128)S(1)}, u32[]{:S(2)}) copy-start(f32[64]{0:T(128)S(1)} %convert_element_type.115) | copy-start | bytes 772
  190.4 188.9 %copy-start.21 = (f32[64]{0:T(128)}, f32[64]{0:T(128)S(1)}, u32[]{:S(2)}) copy-start(f32[64]{0:T(128)S(1)} %convert_element_type.118) | copy-start | bytes 772
  373.7 0.8 copy-start.8
  375.8 6.3 copy-start.14
  378.6 32.7 %copy-start = (bf16[128,1024]{1,0:T(8,128)(2,1)S(1)}, bf16[128,1024]{1,0:T(8,128)(2,1)}, u32[]{:S(2)}) copy-start(bf16[128,1024]{1,0:T(8,128)(2,1)} %param.14) | copy-start | bytes 786436
  379.2 5.4 copy-start.15
  379.3 5.3 copy-start.18
  379.6 33.0 %copy-start.9 = (bf16[4,64,2,128]{3,1,2,0:T(8,128)(2,1)}, bf16[4,64,2,128]{3,1,2,0:T(8,128)(2,1)S(1)}, u32[]{:S(2)}) copy-start(bf16[4,64,2,128]{3,1,2,0:T(8,128)(2,1)S(1)} %convolution_convert_fusion.2) | copy-start | bytes 393220
  382.2 106.6 %all-gather.12.cloned.1.call-start = ((), (), s32[]{:S(2)}) async-start(), calls=%async_computation.5 | async-start | bytes 4792320 | tf_op jit(solution)/shard_map/all_gather | solution.py:150
  382.8 181.0 %all-gather.10.cloned.1.call-start = ((), (), s32[]{:S(2)}) async-start(), calls=%async_computation.4 | async-start | bytes 4792320 | tf_op jit(solution)/shard_map/all_gather | solution.py:149
  383.3 255.3 %all-gather.14.cloned.1.call-start = ((), (), s32[]{:S(2)}) async-start(), calls=%async_computation.6 | async-start | bytes 4792320 | tf_op jit(solution)/shard_map/all_gather | solution.py:152
  383.9 300.2 %all-reduce.20.cloned.1.call-start = ((), (), s32[]{:S(2)}) async-start(), calls=%async_computation.8 | async-start | bytes 1048576 | tf_op jit(solution)/shard_map/psum | solution.py:219
  412.6 0.5 copy-start.23
  413.2 225.5 %copy-start.11 = (bf16[128,1024]{1,0:T(8,128)(2,1)S(1)}, bf16[128,1024]{1,0:T(8,128)(2,1)}, u32[]{:S(2)}) copy-start(bf16[128,1024]{1,0:T(8,128)(2,1)} %param.27) | copy-start | bytes 786436
  638.7 5.1 copy-start.1
  643.8 1.6 copy-start.6
  643.8 1.6 copy-start.4
  650.3 33.8 %copy-start.24 = (f32[128]{0:T(128)S(1)}, f32[128]{0:T(128)}, u32[]{:S(2)}) copy-start(f32[128]{0:T(128)} %copy-done.23) | copy-start | bytes 1540
  650.3 67.6 %all-reduce.18.cloned.1.call-start = ((), (), s32[]{:S(2)}) async-start(), calls=%async_computation.7 | async-start | bytes 524288 | tf_op jit(solution)/shard_map/psum | solution.py:196
  656.5 119.1 %all-reduce.22.cloned.1.call-start = ((), (), s32[]{:S(2)}) async-start(), calls=%async_computation.9 | async-start | bytes 1048576 | tf_op jit(solution)/shard_map/psum | solution.py:244
  721.7 9.7 copy-start.22
  723.6 5.8 copy-start.13
  725.1 9.8 copy-start.17
  730.6 6.3 copy-start.2
  733.6 9.6 copy-start.10
  736.8 8.2 copy-start.7
  739.4 337.8 %reduce-scatter.2.cloned.1.call-start = ((), (), s32[]{:S(2)}) async-start(), calls=%async_computation.10 | async-start | bytes 35143680 | tf_op jit(solution)/shard_map/reduce_scatter | solution.py:253
  745.0 5.1 copy-start.5
  750.1 5.1 copy-start.3
  750.1 5.1 copy-start.12
  760.3 16.6 %copy-start.19 = (f32[1024]{0:T(1024)S(1)}, f32[1024]{0:T(1024)}, u32[]{:S(2)}) copy-start(f32[1024]{0:T(1024)} %get-tuple-element.13) | copy-start | bytes 12292
  760.3 16.6 %copy-start.25 = (f32[64]{0:T(128)S(1)}, f32[64]{0:T(128)}, u32[]{:S(2)}) copy-start(f32[64]{0:T(128)} %get-tuple-element.19) | copy-start | bytes 772
Sparse Core Ops, SparseCore 0:
  11.3 68.3 all-gather.5
  83.1 62.7 all-gather.7
  382.3 28.9 all-reduce.15
  414.9 73.8 all-gather.11
  492.3 71.3 all-gather.9
  567.3 71.3 all-gather.13
  650.4 33.6 all-reduce.19
  687.1 30.7 all-reduce.17
  739.5 36.1 all-reduce.21
  781.9 295.2 reduce-scatter.1
where the time goes:
time: 1090 us
  blocking collectives  535 us (49%)
  waiting for transfers between devices  433 us (40%)
  matrix products  64.5 us (6%)
  other arithmetic  19.2 us (2%)
  local copies, waits for them, and re-layouts  18.9 us (2%)
  between operations  17.3 us (2%)
    unnamed x2, blocking collectives  348 us
    reduce_scatter x1, waiting for transfers between devices, on_device(): lax.psum_scatter(jnp.concatenate([jnp.concatenate([tr_matmul(hidden_one,...  114 us
    all_gather x1, blocking collectives, on_device(): lax.all_gather(shards[2], 'fsdp', axis=0, tiled=True)  91.7 us
    all_gather x1, blocking collectives, on_device(): lax.all_gather(shards[1], 'fsdp', axis=0, tiled=True)  89.9 us
    all_gather x1, waiting for transfers between devices, on_device(): lax.all_gather(shards[4], 'fsdp', axis=0, tiled=True)  75.6 us
    all_gather x1, waiting for transfers between devices, on_device(): lax.all_gather(shards[6], 'fsdp', axis=1, tiled=True)  70.8 us
    all_gather x1, waiting for transfers between devices, on_device(): lax.all_gather(shards[3], 'fsdp', axis=0, tiled=True)  70.8 us
    psum x1, waiting for transfers between devices, on_device(): lax.psum(matmul(activation, full_down).astype(jnp.bfloat16), 'tensor')  31.4 us
  transfers between devices with their start and end apart: 10, of which 8 were waited for; matrix products, arithmetic and copies ran while one was open for 6% of the time, Pallas kernels for 0%

commit v1 on v0

--- a/solution.py
+++ b/solution.py
@@ -142,10 +142,20 @@
         norm_query,
         norm_key,
     )
+
+    def _fix_target(out_dim, z, which_axis):
+        spare = jnp.concatenate(
+            jax.lax.all_to_all(
+                jnp.stack([z] * jax.lax.axis_size(which_axis), axis=0), which_axis, 0, 0
+            ),
+            axis=out_dim,
+        )
+        return spare
+
     gathered = (
         lax.all_gather(shards[0], "fsdp", axis=0, tiled=True),
         lax.all_gather(shards[1], "fsdp", axis=0, tiled=True),
-        lax.all_gather(shards[2], "fsdp", axis=0, tiled=True),
+        _fix_target(0, shards[2], "fsdp"),
         lax.all_gather(shards[3], "fsdp", axis=0, tiled=True),
         lax.all_gather(shards[4], "fsdp", axis=0, tiled=True),
         lax.all_gather(shards[5], "fsdp", axis=1, tiled=True),

time: 1090 us -> 1010 us (0.927)
  blocking collectives: 535 us -> 442 us
  starting transfers between devices: 0.57 us -> 12.1 us
    all_gather x1 -> x0, blocking collectives: 91.7 us -> none  [on_device(): lax.all_gather(shards[2], 'fsdp', axis=0, tiled=True)]
    all_to_all x0 -> x1, starting transfers between devices: none -> 11.5 us  [_fix_target(): jax.lax.all_to_all(jnp.stack([z] * jax.lax.axis_size(which_axis), axis=0)...]
  transfers between devices with their start and end apart: 10 -> 11, of which waited for: 8 -> 8; matrix products, arithmetic and copies ran while one was open for 6% -> 6% of each run, Pallas kernels for 0% -> 0%
where the time goes in v1:
time: 1010 us
  blocking collectives  442 us (44%)
  waiting for transfers between devices  434 us (43%)
  matrix products  64.6 us (6%)
  local copies, waits for them, and re-layouts  19.6 us (2%)
  other arithmetic  19.2 us (2%)
  between operations  17.4 us (2%)
  starting transfers between devices  12.1 us (1%)
    unnamed x2, blocking collectives  347 us
    reduce_scatter x1, waiting for transfers between devices, on_device(): lax.psum_scatter(jnp.concatenate([jnp.concatenate([tr_matmul(hidden_one,...  114 us
    all_gather x1, blocking collectives, on_device(): lax.all_gather(shards[1], 'fsdp', axis=0, tiled=True)  89.9 us
    all_gather x1, waiting for transfers between devices, on_device(): lax.all_gather(shards[4], 'fsdp', axis=0, tiled=True)  75.6 us
    all_gather x1, waiting for transfers between devices, on_device(): lax.all_gather(shards[6], 'fsdp', axis=1, tiled=True)  70.8 us
    all_gather x1, waiting for transfers between devices, on_device(): lax.all_gather(shards[3], 'fsdp', axis=0, tiled=True)  70.8 us
    psum x1, waiting for transfers between devices, on_device(): lax.psum(matmul(activation, full_down).astype(jnp.bfloat16), 'tensor')  31.4 us
    psum x1, waiting for transfers between devices, on_device(): grad_hidden_two = lax.psum(partial_two, 'tensor')  27.3 us
  transfers between devices with their start and end apart: 11, of which 8 were waited for; matrix products, arithmetic and copies ran while one was open for 6% of the time, Pallas kernels for 0%

profile of v1, /device:TPU:0, one launch (start us, length us, event | category | flops | bytes accessed | tf_op | source)
XLA Modules:
  0.0 1009.4 jit_solution(2245898893422974511)
XLA Ops:
  7.9 1.5 stack.2
  9.5 11.5 %all-to-all-start = ((bf16[64,16,256]{2,1,0:T(8,128)(2,1)}), bf16[64,16,256]{2,1,0:T(8,128)(2,1)S(1)}, u32[]{:S(2)}, u32[]{:S(2)}) async-start(bf16[64,16,256]{2,1,0:T(8,128)(2,1)} %stack.2), calls=%async_computation | async-start | bytes 1048576 | tf_op jit(solution)/shard_map/all_to_all | solution.py:148
  25.9 1.3 fusion.45
  31.1 172.0 %all-reduce.10 = (bf16[1024]{0:T(1024)(128)(2,1)S(1)}, bf16[64]{0:T(256)(128)(2,1)S(1)}, bf16[64]{0:T(256)(128)(2,1)S(1)}, bf16[1024]{0:T(1024)(128)(2,1)S(1)}) all-reduce(bf16[1024]{0:T(1024)(128)(2,1)S(1)} %dynamic-update-slice, bf16[64]{0:T(256)(128)(2,1)S(1)} %dynamic-update-slice.1, ...), channel_id=1, replica_groups=mesh['fsdp'=64,'tensor'=2] {'fsdp'}, use_global_device_ids=true, to_apply=%add | all-reduce | flops 2176 | bytes 8704
  203.1 89.9 %all_gather.31 = bf16[1024,256]{1,0:T(8,128)(2,1)S(1)} all-gather(bf16[16,256]{1,0:T(8,128)(2,1)} %param.17), channel_id=1, replica_groups=mesh['fsdp'=64,'tensor'=2] {'fsdp'}, dimensions={0}, use_global_device_ids=true | all-gather | bytes 532480 | tf_op jit(solution)/shard_map/all_gather | solution.py:157
  293.0 1.4 multiply_reduce_fusion.9
  294.7 1.4 convolution_convert_fusion.3
  296.3 1.6 fusion.37
  299.1 2.5 fusion.47
  305.8 26.3 %all-reduce.16.cloned.1.call-done = f32[128,1024]{1,0:T(8,128)} async-done(((f32[128,1024]{1,0:T(8,128)}), f32[128,1024]{1,0:T(8,128)}) %all-reduce.16.cloned.1.call-update) | async-done | bytes 524304 | tf_op jit(solution)/shard_map/psum | solution.py:199
  332.1 1.2 multiply_reduce_fusion.2
  334.0 75.6 %all-gather.12.cloned.1.call-done = bf16[1024,2304]{1,0:T(8,128)(2,1)} async-done(((bf16[16,2304]{1,0:T(8,128)(2,1)}), bf16[1024,2304]{1,0:T(8,128)(2,1)}) %all-gather.12.cloned.1.call-update) | async-done | bytes 4718608 | tf_op jit(solution)/shard_map/all_gather | solution.py:160
  409.6 4.2 fusion.49
  413.7 70.8 %all-gather.10.cloned.1.call-done = bf16[1024,2304]{1,0:T(8,128)(2,1)} async-done(((bf16[16,2304]{1,0:T(8,128)(2,1)}), bf16[1024,2304]{1,0:T(8,128)(2,1)}) %all-gather.10.cloned.1.call-update) | async-done | bytes 4718608 | tf_op jit(solution)/shard_map/all_gather | solution.py:159
  484.5 4.2 fusion.48
  488.7 70.8 %all-gather.14.cloned.1.call-done = bf16[2304,1024]{0,1:T(8,128)(2,1)} async-done(((bf16[2304,16]{0,1:T(8,128)(2,1)}), bf16[2304,1024]{0,1:T(8,128)(2,1)}) %all-gather.14.cloned.1.call-update) | async-done | bytes 4718608 | tf_op jit(solution)/shard_map/all_gather | solution.py:162
  559.5 5.1 multiply_convert_fusion
  564.6 1.6 fusion.50
  566.3 4.8 convolution_add_fusion.1
  571.1 1.3 log_add_fusion
  572.4 4.9 convolution_convert_fusion
  577.6 27.3 %all-reduce.20.cloned.1.call-done = f32[128,1024]{1,0:T(8,128)} async-done(((f32[128,1024]{1,0:T(8,128)}), f32[128,1024]{1,0:T(8,128)}) %all-reduce.20.cloned.1.call-update) | async-done | bytes 524304 | tf_op jit(solution)/shard_map/psum | solution.py:229
  604.9 1.9 multiply_reduce_fusion
  607.3 31.4 %all-reduce.18.cloned.1.call-done = bf16[128,1024]{1,0:T(8,128)(2,1)} async-done(((bf16[128,1024]{1,0:T(8,128)(2,1)}), bf16[128,1024]{1,0:T(8,128)(2,1)}) %all-reduce.18.cloned.1.call-update) | async-done | bytes 262160 | tf_op jit(solution)/shard_map/psum | solution.py:206
  638.7 2.2 multiply_add_fusion
  640.8 1.5 convolution_convert_fusion.1
  645.9 2.1 fusion.53
  648.1 1.4 multiply_reduce_fusion.7
  654.4 1.3 multiply_convert_fusion.4
  655.7 1.9 convolution_dynamic-update-slice_fusion.3
  657.7 2.5 fusion
  660.3 1.4 convolution_dynamic-update-slice_fusion.5
  661.7 2.3 convolution_dynamic-update-slice_fusion.4
  664.0 1.8 convolution_dynamic-update-slice_fusion.2
  665.8 5.0 convolution_dynamic-update-slice_fusion.1
  670.8 5.0 convolution_dynamic-update-slice_fusion
  675.8 5.2 bitcast_dynamic-update-slice_fusion
  681.1 15.4 %all-reduce.22.cloned.1.call-done = f32[128,1024]{1,0:T(8,128)} async-done(((f32[128,1024]{1,0:T(8,128)}), f32[128,1024]{1,0:T(8,128)}) %all-reduce.22.cloned.1.call-update) | async-done | bytes 524304 | tf_op jit(solution)/shard_map/psum | solution.py:254
  696.5 1.3 fusion.18
  697.8 174.7 %all-reduce.8 = (f32[1024]{0:T(1024)S(1)}, f32[1024]{0:T(1024)S(1)}, f32[64]{0:T(128)S(1)}, f32[64]{0:T(128)S(1)}) all-reduce(f32[1024]{0:T(1024)S(1)} %get-tuple-element.15, f32[1024]{0:T(1024)S(1)} %copy-done.19, f32[64]{0:T(128)S(1)} %get-tuple-element.17, f32[64]{0:T(128)S(1)} %copy-done.25), channel_id=3, replica_groups=mesh['fsdp'=64,'tensor'=2] {'fsdp'}, use_global_device_ids=true, to_apply=%region_18.19.clone | all-reduce | flops 2176 | bytes 17408
  872.5 1.2 dynamic-slice.11
  873.8 1.2 dynamic-slice.9
  875.7 5.6 all-reduce.9
  882.4 2.0 fusion.17
  884.4 113.6 %reduce-scatter.2.cloned.1.call-done = f32[16,8448]{1,0:T(8,128)} async-done(((f32[1024,8448]{1,0:T(8,128)}), f32[16,8448]{1,0:T(8,128)}) %reduce-scatter.2.cloned.1.call-update) | async-done | bytes 540688 | tf_op jit(solution)/shard_map/reduce_scatter | solution.py:263
  998.0 1.3 fusion.42
  999.4 1.4 slice_bitcast_fusion.1
  1000.8 1.8 slice_bitcast_fusion
  (140 shorter events, 24.2 us)
Async XLA Ops:
  7.2 289.2 %copy-start = (bf16[128,1024]{1,0:T(8,128)(2,1)S(1)}, bf16[128,1024]{1,0:T(8,128)(2,1)}, u32[]{:S(2)}) copy-start(bf16[128,1024]{1,0:T(8,128)(2,1)} %param.14) | copy-start | bytes 786436
  7.2 289.1 %all-gather.6.cloned.1.call-start = ((), (), s32[]{:S(2)}) async-start(), calls=%async_computation.2 | async-start | bytes 1064960 | tf_op jit(solution)/shard_map/all_gather | solution.py:156
  9.5 285.3 %all-to-all-start = ((bf16[64,16,256]{2,1,0:T(8,128)(2,1)}), bf16[64,16,256]{2,1,0:T(8,128)(2,1)S(1)}, u32[]{:S(2)}, u32[]{:S(2)}) async-start(bf16[64,16,256]{2,1,0:T(8,128)(2,1)} %stack.2), calls=%async_computation | async-start | bytes 1048576 | tf_op jit(solution)/shard_map/all_to_all | solution.py:148
  21.0 278.1 %all-gather.8.cloned.1.call-start = ((), (), s32[]{:S(2)}) async-start(), calls=%async_computation.3 | async-start | bytes 1064960 | tf_op jit(solution)/shard_map/all_gather | solution.py:161
  21.7 310.4 %all-reduce.16.cloned.1.call-start = ((), (), s32[]{:S(2)}) async-start(), calls=%async_computation.4 | async-start | bytes 1048576 | tf_op jit(solution)/shard_map/psum | solution.py:199
  25.9 272.2 %copy-start.16 = (f32[128]{0:T(128)}, f32[128]{0:T(128)S(1)}, u32[]{:S(2)}) copy-start(f32[128]{0:T(128)S(1)} %add_rsqrt_fusion.3) | copy-start | bytes 1540
  203.1 95.2 %copy-start.20 = (f32[64]{0:T(128)}, f32[64]{0:T(128)S(1)}, u32[]{:S(2)}) copy-start(f32[64]{0:T(128)S(1)} %convert_element_type.117) | copy-start | bytes 772
  294.6 4.2 copy-start.21
  294.7 1.6 copy-start.8
  296.3 5.3 copy-start.14
  298.6 5.4 copy-start.15
  298.8 5.3 copy-start.18
  299.0 34.3 %copy-start.9 = (bf16[4,64,2,128]{3,1,2,0:T(8,128)(2,1)}, bf16[4,64,2,128]{3,1,2,0:T(8,128)(2,1)S(1)}, u32[]{:S(2)}) copy-start(bf16[4,64,2,128]{3,1,2,0:T(8,128)(2,1)S(1)} %convolution_convert_fusion.2) | copy-start | bytes 393220
  301.6 107.9 %all-gather.12.cloned.1.call-start = ((), (), s32[]{:S(2)}) async-start(), calls=%async_computation.6 | async-start | bytes 4792320 | tf_op jit(solution)/shard_map/all_gather | solution.py:160
  302.2 182.3 %all-gather.10.cloned.1.call-start = ((), (), s32[]{:S(2)}) async-start(), calls=%async_computation.5 | async-start | bytes 4792320 | tf_op jit(solution)/shard_map/all_gather | solution.py:159
  302.8 256.7 %all-gather.14.cloned.1.call-start = ((), (), s32[]{:S(2)}) async-start(), calls=%async_computation.7 | async-start | bytes 4792320 | tf_op jit(solution)/shard_map/all_gather | solution.py:162
  303.4 301.5 %all-reduce.20.cloned.1.call-start = ((), (), s32[]{:S(2)}) async-start(), calls=%async_computation.9 | async-start | bytes 1048576 | tf_op jit(solution)/shard_map/psum | solution.py:229
  333.3 0.5 copy-start.23
  334.0 225.5 %copy-start.11 = (bf16[128,1024]{1,0:T(8,128)(2,1)S(1)}, bf16[128,1024]{1,0:T(8,128)(2,1)}, u32[]{:S(2)}) copy-start(bf16[128,1024]{1,0:T(8,128)(2,1)} %param.27) | copy-start | bytes 786436
  559.5 5.2 copy-start.1
  564.6 1.6 copy-start.6
  564.6 1.6 copy-start.4
  571.1 33.8 %copy-start.24 = (f32[128]{0:T(128)S(1)}, f32[128]{0:T(128)}, u32[]{:S(2)}) copy-start(f32[128]{0:T(128)} %copy-done.23) | copy-start | bytes 1540
  571.1 67.6 %all-reduce.18.cloned.1.call-start = ((), (), s32[]{:S(2)}) async-start(), calls=%async_computation.8 | async-start | bytes 524288 | tf_op jit(solution)/shard_map/psum | solution.py:206
  577.3 119.2 %all-reduce.22.cloned.1.call-start = ((), (), s32[]{:S(2)}) async-start(), calls=%async_computation.10 | async-start | bytes 1048576 | tf_op jit(solution)/shard_map/psum | solution.py:254
  642.5 9.7 copy-start.22
  644.4 5.8 copy-start.13
  645.9 9.8 copy-start.17
  651.3 6.3 copy-start.2
  654.4 9.6 copy-start.10
  657.7 8.1 copy-start.7
  660.2 337.8 %reduce-scatter.2.cloned.1.call-start = ((), (), s32[]{:S(2)}) async-start(), calls=%async_computation.11 | async-start | bytes 35143680 | tf_op jit(solution)/shard_map/reduce_scatter | solution.py:263
  665.8 5.0 copy-start.5
  670.8 5.0 copy-start.3
  670.8 5.0 copy-start.12
  681.0 16.8 %copy-start.19 = (f32[1024]{0:T(1024)S(1)}, f32[1024]{0:T(1024)}, u32[]{:S(2)}) copy-start(f32[1024]{0:T(1024)} %get-tuple-element.13) | copy-start | bytes 12292
  681.0 16.8 %copy-start.25 = (f32[64]{0:T(128)S(1)}, f32[64]{0:T(128)}, u32[]{:S(2)}) copy-start(f32[64]{0:T(128)} %get-tuple-element.19) | copy-start | bytes 772
Sparse Core Ops, SparseCore 0:
  11.4 68.9 all-gather.5
  83.6 62.6 all-gather.7
  301.7 30.3 all-reduce.15
  335.6 73.8 all-gather.11
  413.1 71.3 all-gather.9
  488.0 71.3 all-gather.13
  571.2 33.6 all-reduce.19
  607.9 30.7 all-reduce.17
  660.3 36.1 all-reduce.21
  702.8 295.2 reduce-scatter.1
